TPU v7x, 128 devices: a whole 4x4x4 slice. The times are simulated.
128 devices in a mesh: req: 16 (over y, x), seq: 4 (over z), hid: 2 (over core).
Axes of the slice: x: 4, y: 4, z: 4, core: 2. Of those that a mesh axis runs over, the one named last changes fastest.
Arguments:
- tokens: bfloat16 [65536, 2048], P(('req', 'seq')), may hold values from -6 to 6
- attention_gain: bfloat16 [2048], replicated, may hold values from 0.099609375 to 1.8984375
- project_weight: bfloat16 [2048, 2048], P(None, 'hid'), may hold values from -0.125 to 0.125
- conv_weight: bfloat16 [4, 2048], P(None, 'hid'), may hold values from -3 to 3
- decay_down: bfloat16 [2048, 16], replicated, may hold values from -0.125 to 0.125
- decay_up: bfloat16 [16, 512], P(None, 'hid'), may hold values from -1.5 to 1.5
- decay_bias: float32 [512], P('hid'), may hold values from -2 to 10
- output_gate: bfloat16 [2048, 1024], P(None, 'hid'), may hold values from -0.125 to 0.125
- head_gain: bfloat16 [512], replicated, may hold values from 0.099609375 to 1.8984375
- output_weight: bfloat16 [1024, 2048], P('hid'), may hold values from -0.1875 to 0.1875
- mixer_gain: bfloat16 [2048], replicated, may hold values from 0.099609375 to 1.8984375
- gate_weight: bfloat16 [2048, 2816], P('req', 'hid'), may hold values from -0.125 to 0.125
- up_weight: bfloat16 [2048, 2816], P('req', 'hid'), may hold values from -0.125 to 0.125
- down_weight: bfloat16 [2816, 2048], P('hid', 'req'), may hold values from -0.109375 to 0.109375
- prompt_pages: int32 [16, 16], P('req'), may hold values from 0 to 64, as said below
- prompt_start: int32 [16, 16], P('req'), may hold values from 0 to 63, as said below
Outputs:
- hidden_out: bfloat16 [65536, 2048], P(('req', 'seq', 'hid'))
- page_states: bfloat16 [1024, 2, 256, 512], P(('req', 'seq'), 'hid')
- conv_edges: bfloat16 [1024, 3, 2048], P(('req', 'seq'), None, 'hid')
Inputs may be any that keep to these rules, and one draw needn't show every extreme that they name: `prompt_pages`: row r lists the page counts of the prompts of group r; 0 marks an unused slot; in every draw some group holds one prompt of all its 64 pages. `prompt_start`: the slots of a row that are used cover pages in increasing order without intersection and end by page 64; pages between prompts belong to none; an unused slot starts at page 64 - 1, and every draw has one.
All inputs are finite; a program needn't handle non-finite values.
Results may differ from a plain program's by a relative error of at most 0.014.
Values may be sent and summed in bfloat16 or wider, within the bound.
A program may use at most 192 MiB of HBM per device.

v0:
```python
import jax
import jax.numpy as jnp
from jax import lax
from jax.sharding import PartitionSpec as P

HK = 256
HV = 512
KCONV = 4
PAGE = 64
CONVW = 1024
EPSILON = 1e-06
TOP_PRECISION = lax.Precision.HIGHEST


def shifted(value, axis, steps):
    count = lax.axis_size(axis)
    first, last = (max(0, -steps), min(count, count - steps))
    return lax.ppermute(value, axis, [(source, source + steps) for source in range(first, last)])


def prefix_2(array, axis, join, neutral):
    place = lax.axis_index(axis)
    gathered = jax.tree.map(
        lambda a, kind: lax.all_gather(a.astype(kind), axis), array, (jnp.bfloat16, jnp.bfloat16)
    )
    state = jax.tree.map(lambda a, e: jnp.zeros_like(a) + jnp.asarray(e, a.dtype), array, neutral)

    def one(lap, state):
        return join(
            state,
            jax.tree.map(
                lambda a, own: lax.dynamic_index_in_dim(a, lap, 0, False).astype(own.dtype),
                gathered,
                array,
            ),
        )

    return lax.fori_loop(0, place, one, state)


def rms_scaled(values, scale_gain):
    values = values.astype(jnp.float32)
    return (
        values
        * lax.rsqrt(jnp.mean(values * values, axis=-1, keepdims=True) + EPSILON)
        * scale_gain.astype(jnp.float32)
    )


def page_segments(page_counts, starts, total_pages):
    position = jnp.arange(total_pages, dtype=jnp.int32)
    inside = (position[None, :] >= starts[:, None]) & (
        position[None, :] < starts[:, None] + page_counts[:, None]
    )
    labels = jnp.arange(1, page_counts.shape[0] + 1, dtype=jnp.int32)
    segment = jnp.sum(jnp.where(inside, labels[:, None], 0), axis=0) - 1
    earlier = jnp.concatenate([jnp.full((1,), -1, jnp.int32), segment[:-1]])
    return ((segment == earlier) & (segment >= 0)).astype(jnp.float32)


def short_conv(by_page, before, carried, conv_taps):
    kept_rows = before.astype(jnp.float32) * carried[:, None, None]
    widened = jnp.concatenate([kept_rows, by_page.astype(jnp.float32)], axis=1)
    tap_count = conv_taps.shape[0]
    length = by_page.shape[1]
    result = jnp.zeros(by_page.shape, jnp.float32)
    for offset in range(tap_count):
        result = (
            result
            + conv_taps[offset].astype(jnp.float32)
            * widened[:, tap_count - 1 - offset : tap_count - 1 - offset + length]
        )
    return result


def split_features(mixed_rows, key_width):
    query_rows = jax.nn.silu(mixed_rows[..., :key_width])
    key_rows = jax.nn.silu(mixed_rows[..., key_width : 2 * key_width]) * key_width ** (-0.5)
    value_matrix = mixed_rows[..., 2 * key_width :]
    return (
        query_rows.transpose(0, 2, 1, 3),
        key_rows.transpose(0, 2, 1, 3),
        value_matrix.transpose(0, 2, 1, 3),
    )


def page_block(query_rows, key_rows, value_matrix, decay_sum, carried):
    length = query_rows.shape[2]
    page_count = query_rows.shape[0]
    raised_rows = query_rows * jnp.exp(decay_sum)
    lowered = key_rows * jnp.exp(-decay_sum)
    scores = jnp.einsum("phik,phjk->phij", raised_rows, lowered, precision=TOP_PRECISION)
    rows_index = jnp.arange(length)
    causal = rows_index[:, None] >= rows_index[None, :]
    scores = jnp.where(causal[None, None], scores, 0.0)
    layer_output = jnp.einsum("phij,phjv->phiv", scores, value_matrix, precision=TOP_PRECISION)
    closing_sum = decay_sum[:, :, -1, :]
    weighted_rows = key_rows * jnp.exp(closing_sum[:, :, None, :] - decay_sum)
    page_terms = jnp.einsum("phte,phtb->pheb", weighted_rows, value_matrix, precision=TOP_PRECISION)
    through = jnp.cumsum(closing_sum, axis=0)
    resets = jnp.cumsum(1.0 - carried)
    pages = jnp.arange(page_count)
    valid = (pages[:, None] >= pages[None, :]) & (resets[:, None] == resets[None, :])
    spread = through[:, None] - through[None, :]
    spread = jnp.where(valid[:, :, None, None], spread, 0.0)
    weights = jnp.where(valid[:, :, None, None], jnp.exp(spread), 0.0)
    memories = jnp.einsum("pqhe,qheb->pheb", weights, page_terms, precision=TOP_PRECISION)
    previous = jnp.concatenate([jnp.zeros_like(memories[:1]), memories[:-1]], axis=0)
    previous = previous * carried[:, None, None, None]
    layer_output = layer_output + jnp.einsum(
        "phik,phkv->phiv", raised_rows, previous, precision=TOP_PRECISION
    )
    return (memories[-1], layer_output, memories)


def on_device(
    tokens,
    attention_gain,
    project_weight,
    conv_weight,
    decay_down,
    decay_up,
    decay_bias,
    output_gate,
    head_gain,
    output_weight,
    mixer_gain,
    gate_weight,
    up_weight,
    down_weight,
    prompt_pages,
    prompt_start,
):
    token_count = tokens.shape[0]
    page_count = token_count // PAGE
    local_heads = project_weight.shape[1] // CONVW
    rim_rows = KCONV - 1
    seq_index = lax.axis_index("seq")
    group_pages = page_count * lax.axis_size("seq")
    page_flags = page_segments(prompt_pages[0], prompt_start[0], group_pages)
    carried = lax.dynamic_slice_in_dim(page_flags, seq_index * page_count, page_count)
    normed = rms_scaled(tokens, attention_gain).astype(jnp.bfloat16)
    projected = jnp.dot(normed, project_weight, preferred_element_type=jnp.float32).astype(
        jnp.bfloat16
    )
    by_page = projected.reshape(page_count, PAGE, local_heads * CONVW)
    incoming = shifted(by_page[-1, PAGE - rim_rows :], "seq", 1)
    before = jnp.concatenate([incoming[None], by_page[:-1, PAGE - rim_rows :]], axis=0)
    mixed_rows = short_conv(by_page, before, carried, conv_weight).reshape(
        page_count, PAGE, local_heads, CONVW
    )
    query_rows, key_rows, value_matrix = split_features(mixed_rows, HK)
    lowrank = jnp.dot(normed, decay_down, preferred_element_type=jnp.float32).astype(jnp.bfloat16)
    decay_log = (
        jax.nn.log_sigmoid(
            jnp.dot(lowrank, decay_up, preferred_element_type=jnp.float32) + decay_bias
        )
        / 16.0
    )
    decay_log = decay_log.reshape(page_count, PAGE, local_heads, HK).transpose(0, 2, 1, 3)
    decay_sum = jnp.cumsum(decay_log, axis=2)
    local_memory, outputs, memories = page_block(
        query_rows, key_rows, value_matrix, decay_sum, carried
    )
    totals = decay_sum[:, :, -1, :]
    through = jnp.cumsum(totals, axis=0)
    alive_mask = jnp.cumprod(carried)
    block_decay = alive_mask[-1] * jnp.exp(through[-1])

    def compose(earlier, latter):
        return (earlier[0] * latter[0], latter[0][..., None] * earlier[1] + latter[1])

    prefix = prefix_2(
        (block_decay, local_memory),
        "seq",
        compose,
        (jnp.ones_like(block_decay), jnp.zeros_like(local_memory)),
    )
    incoming_state = prefix[1]
    before_sum = through - totals
    extent_factor = alive_mask[:, None, None, None] * jnp.exp(decay_sum + before_sum[:, :, None, :])
    outputs = outputs + jnp.einsum(
        "dlof,lfg->dlog", query_rows * extent_factor, incoming_state, precision=TOP_PRECISION
    )
    memories = (
        memories + (alive_mask[:, None, None] * jnp.exp(through))[..., None] * incoming_state[None]
    )
    attended = outputs.transpose(0, 2, 1, 3).reshape(token_count, local_heads, HV)
    normed_heads = rms_scaled(attended, head_gain)
    opening = jax.nn.silu(jnp.dot(normed, output_gate, preferred_element_type=jnp.float32)).reshape(
        token_count, local_heads, HV
    )
    gated_rows = (
        (normed_heads * opening).astype(jnp.bfloat16).reshape(token_count, local_heads * HV)
    )
    partial_value = jnp.dot(gated_rows, output_weight, preferred_element_type=jnp.float32)
    half_rows = token_count // lax.axis_size("hid")
    row_start = lax.axis_index("hid") * half_rows
    mixed_sum = lax.psum(partial_value.astype(jnp.bfloat16), "hid").astype(jnp.float32)
    residual = (tokens.astype(jnp.float32) + mixed_sum).astype(jnp.bfloat16)
    feed_in = rms_scaled(residual, mixer_gain).astype(jnp.bfloat16)
    own_residual = lax.dynamic_slice_in_dim(residual, row_start, half_rows, 0)

    def widen(weight_rows):
        return jnp.dot(feed_in, weight_rows, preferred_element_type=jnp.float32)

    gate_part = widen(lax.all_gather(gate_weight, "req", axis=0, tiled=True))
    up_part = widen(lax.all_gather(up_weight, "req", axis=0, tiled=True))
    hidden = (jax.nn.silu(gate_part) * up_part).astype(jnp.bfloat16)
    partials = jnp.dot(
        hidden,
        lax.all_gather(down_weight, "req", axis=1, tiled=True),
        preferred_element_type=jnp.float32,
    )
    feed_sum = lax.psum_scatter(
        partials.astype(jnp.bfloat16), "hid", scatter_dimension=0, tiled=True
    ).astype(jnp.float32)
    result = (own_residual.astype(jnp.float32) + feed_sum).astype(jnp.bfloat16)
    return (result, memories.astype(jnp.bfloat16), by_page[:, PAGE - rim_rows :])


def solution(mesh):
    return jax.shard_map(
        on_device,
        mesh=mesh,
        in_specs=(
            P(("req", "seq"), None),
            P(),
            P(None, "hid"),
            P(None, "hid"),
            P(),
            P(None, "hid"),
            P("hid"),
            P(None, "hid"),
            P(),
            P("hid", None),
            P(),
            P("req", "hid"),
            P("req", "hid"),
            P("hid", "req"),
            P("req", None),
            P("req", None),
        ),
        out_specs=(
            P(("req", "seq", "hid"), None),
            P(("req", "seq"), "hid", None, None),
            P(("req", "seq"), None, "hid"),
        ),
        check_vma=False,
    )
```

profile of v0, /device:TPU:1, one launch (start us, length us, event | category | flops | bytes accessed | tf_op | source)
XLA Modules:
  0.0 364.4 jit_solution(5683534701682440027)
XLA Ops:
  8.0 0.0 copy-start
  8.0 0.0 all-gather.5.cloned.1.call-start
  8.1 3.2 fusion.3
  11.3 0.3 copy-done.6
  11.7 7.3 %convolution_convert_fusion.2 = bf16[1024,1024]{1,0:T(8,128)(2,1)S(1)} fusion(bf16[2048,1024]{1,0:T(8,128)(2,1)} %param.20, bf16[1024,2048]{1,0:T(8,128)(2,1)S(1)} %copy-done.6, f32[2048]{0:T(1024)S(1)} %convert_element_type.149, f32[1024]{0:T(1024)S(1)} %add_rsqrt_fusion.2), kind=kOutput, calls=%fused_computation.53 | convolution fusion | flops 4304404480 | bytes 10498048 | tf_op jit(solution)/shard_map/dot_general | solution.py:143
  19.0 1.3 copy-done.7
  20.3 4.4 %collective-permute-start = (bf16[3,1024]{1,0:T(4,128)(2,1)S(1)}, bf16[3,1024]{1,0:T(4,128)(2,1)S(1)}, u32[]{:S(2)}, u32[]{:S(2)}) collective-permute-start(bf16[3,1024]{1,0:T(4,128)(2,1)S(1)} %slice_bitcast_fusion.5), channel_id=1, source_target_pairs={{0,2},{2,4},{4,6},{1,3},{3,5},{5,7},{8,10},{10,12},{12,14},{9,11},... | collective-permute-start | bytes 18440 | tf_op jit(solution)/shard_map/ppermute | solution.py:18
  24.7 0.1 select_reduce_fusion
  24.9 5.2 %fusion.37 = f32[1024,256]{1,0:T(8,128)} fusion(bf16[16,256]{1,0:T(8,128)(2,1)S(1)} %copy-done.15, bf16[2048,16]{0,1:T(8,128)(2,1)S(1)} %copy-done.14, f32[256]{0:T(256)S(1)} %copy-done.16, bf16[1024,2048]{1,0:T(8,128)(2,1)} %param.18, f32[2048]{0:T(1024)S(1)} %convert_element_type.149, f32[1024]{0:T(1024)S(1)} %add_rsqrt_fusion.2), kind=kOutput, calls=%fused_computation.60 | convolution fusion | flops 86523904 | bytes 5329920 | tf_op jit(solution)/shard_map/dot_general | solution.py:156
  30.0 1.8 fusion.48
  31.9 0.1 and_convert_fusion
  32.0 0.1 subtract_bitcast_fusion
  32.1 0.1 copy.61
  32.2 0.1 reduce.2
  32.3 0.1 fusion.69
  32.4 0.1 copy.67
  32.5 0.5 slice.90
  33.1 0.7 fusion.71
  33.7 1.0 slice.80
  34.8 4.1 %convert_element_type.152 = f32[16,64,1024]{2,1,0:T(8,128)} convert(bf16[16,64,1024]{2,1,0:T(8,128)(2,1)} %bitcast.138) | non-fusion elementwise | flops 1048576 | bytes 6291456 | tf_op jit(solution)/shard_map/convert_element_type | solution.py:63
  38.8 0.1 copy.75
  38.9 0.1 reduce.3
  39.1 6.9 %all_gather.17 = bf16[4,1,256]{2,1,0:T(2,128)(2,1)S(1)} all-gather(bf16[1,1,256]{2,1,0:T(2,128)(2,1)S(1)} %fusion.71), channel_id=1, replica_groups=mesh['req'=16,'seq'=4,'hid'=2] {'seq'}, dimensions={0}, use_global_device_ids=true | all-gather | bytes 2560 | tf_op jit(solution)/shard_map/all_gather | solution.py:24
  46.0 0.1 convert_multiply_fusion.4
  46.1 7.6 %fusion.15 = f32[16,64,1,1024]{3,1,0,2:T(8,128)S(1)} fusion(f32[16,64,1024]{2,1,0:T(8,128)} %convert_element_type.152, f32[16,3,1024]{2,1,0:T(4,128)S(1)} %convert_multiply_fusion.4, f32[1024]{0:T(1024)S(1)} %bitcast.145, f32[1024]{0:T(1024)S(1)} %bitcast.146, f32[1024]{0:T(1024)S(1)} %bitcast.144, f32[1024]{0:T(1024)S(1)} %bitcast.143), kind=kLoop, calls=%fused_computation.29 | loop fusion | flops 10485760 | bytes 8601600 | tf_op jit(solution)/shard_map/reshape | solution.py:149
  53.7 7.4 %fusion.30 = f32[16,256,512]{2,1,0:T(8,128)S(1)} fusion(f32[16,64,1,1024]{3,1,0,2:T(8,128)S(1)} %fusion.15, f32[16,1,64,256]{3,0,1,2:T(8,128)S(1)} %fusion.48, f32[16,256]{1,0:T(8,128)S(1)} %get-tuple-element.85), kind=kOutput, calls=%fused_computation.51 | convolution fusion | flops 1612447744 | bytes 12599296 | tf_op jit(solution)/shard_map/phte,phtb->pheb/dot_general | solution.py:99
  61.1 13.6 %fusion.20 = f32[16,1,256,512]{3,0,2,1:T(8,128)S(1)} fusion(f32[16,256,512]{2,1,0:T(8,128)S(1)} %fusion.30, f32[16,256]{0,1:T(8,128)S(1)} %bitcast.140, pred[16,16]{1,0:T(8,128)(4,1)S(1)} %fusion.69), kind=kOutput, calls=%fused_computation.38 | convolution fusion | flops 402849792 | bytes 16793856 | tf_op jit(solution)/shard_map/pqhe,qheb->pheb/dot_general | solution.py:107
  74.7 3.2 copy-done.2
  78.0 0.6 slice.154
  78.5 0.8 copy.68
  79.3 0.0 all-gather.5.cloned.1.call-update
  79.3 0.2 all-reduce.3.cloned.1.call-start
  79.5 4.2 %convolution_select_fusion = f32[16,64,64]{2,1,0:T(8,128)S(1)} fusion(f32[16,1,64,256]{3,0,1,2:T(8,128)S(1)} %fusion.48, pred[64,64]{1,0:T(8,128)(4,1)S(1)} %iota_compare_fusion, f32[16,64,1,1024]{3,1,0,2:T(8,128)} %copy-done.3), kind=kOutput, calls=%fused_computation.56 | convolution fusion | flops 204537856 | bytes 4464640 | tf_op jit(solution)/shard_map/phik,phjk->phij/dot_general | solution.py:92
  83.8 3.1 fusion.31
  86.9 5.3 %multiply_bitcast_fusion = f32[16,256,512]{2,0,1:T(8,128)S(1)} fusion(f32[15,1,256,512]{3,0,2,1:T(8,128)} %bitcast.134, f32[16]{0:T(128)S(1)} %get-tuple-element.83), kind=kLoop, calls=%fused_computation.19 | loop fusion | flops 2097152 | bytes 16252992 | tf_op jit(solution)/shard_map/reshape.33
  92.3 13.1 %fusion.7 = f32[16,64,512]{2,1,0:T(8,128)} fusion(f32[16,256,512]{2,0,1:T(8,128)S(1)} %multiply_bitcast_fusion, f32[16,1,64,256]{3,0,1,2:T(8,128)S(1)} %fusion.48, f32[16,64,1,1024]{3,1,0,2:T(8,128)} %copy-done.3), kind=kOutput, calls=%fused_computation.14 | convolution fusion | flops 1611923456 | bytes 12582912 | tf_op jit(solution)/shard_map/phik,phkv->phiv/dot_general | solution.py:110
  105.5 6.8 %multiply_reduce_fusion = (f32[16,64]{1,0:T(8,128)S(1)}, f32[16,1,64,512]{3,2,0,1:T(8,128)}) fusion(f32[16,1,64,256]{3,0,1,2:T(8,128)} %copy-done.5, f32[16,256]{1,0:T(8,128)S(1)} %get-tuple-element.84, f32[16]{0:T(128)S(1)} %reduce.3, f32[16,64,1,1024]{3,1,0,2:T(8,128)} %copy-done.3, f32[1,256,512]{2,1,0:T(8,128)S(1)} %get-tuple-element.47, ...), kind=kOutput, calls=%fused_computation.46 | convolution fusion | flops 1614543872 | bytes 8933440 | tf_op jit(solution)/shard_map/dlof,lfg->dlog/dot_general | solution.py:182
  112.3 0.1 rsqrt.29
  112.4 6.2 %fusion.25 = bf16[1024,512]{1,0:T(8,128)(2,1)S(1)} fusion(f32[16,1,64,512]{3,2,0,1:T(8,128)} %get-tuple-element.91, f32[512]{0:T(512)S(1)} %convert_element_type.163, f32[1024]{0:T(1024)S(1)} %rsqrt.29, bf16[2048,512]{1,0:T(8,128)(2,1)} %param.25, bf16[1024,2048]{1,0:T(8,128)(2,1)} %param.18, f32[2048]{0:T(1024)S(1)} %convert_element_type.149, ...), kind=kOutput, calls=%fused_computation.45 | convolution fusion | flops 2160066560 | bytes 9455616 | tf_op jit(solution)/shard_map/dot_general | solution.py:190
  118.5 4.4 %convolution_convert_fusion.1 = bf16[1024,2048]{1,0:T(8,128)(2,1)} fusion(bf16[1024,512]{1,0:T(8,128)(2,1)S(1)} %fusion.25, bf16[512,2048]{1,0:T(8,128)(2,1)S(1)} %copy-done), kind=kOutput, calls=%fused_computation.37 | convolution fusion | flops 2149580800 | bytes 7340032 | tf_op jit(solution)/shard_map/dot_general | solution.py:196
  122.9 0.0 all-reduce.3.cloned.1.call-update
  122.9 0.0 all-gather.7.cloned.1.call-start
  123.0 0.5 all-gather.7.cloned.1.call-update
  123.5 0.0 all-gather.11.cloned.1.call-start
  123.5 0.5 all-gather.11.cloned.1.call-update
  124.1 0.0 all-gather.9.cloned.1.call-start
  124.1 0.5 all-gather.9.cloned.1.call-update
  124.7 0.3 reduce-scatter.2.cloned.1.call-start
  125.0 37.7 %all-reduce.3.cloned.1.call-done = bf16[1024,2048]{1,0:T(8,128)(2,1)} async-done(((bf16[1024,2048]{1,0:T(8,128)(2,1)}), bf16[1024,2048]{1,0:T(8,128)(2,1)}) %all-reduce.3.cloned.1.call-update) | async-done | bytes 4194320 | tf_op jit(solution)/shard_map/psum | solution.py:199
  162.7 7.7 %fusion = (f32[1024]{0:T(1024)S(1)}, bf16[1024,2048]{1,0:T(8,128)(2,1)}) fusion(bf16[1024,2048]{1,0:T(8,128)(2,1)} %all-reduce.3.cloned.1.call-done, bf16[1024,2048]{1,0:T(8,128)(2,1)} %param.18), kind=kLoop, calls=%fused_computation.7 | loop fusion | flops 14679040 | bytes 12587008 | tf_op jit(solution)/shard_map/reduce_sum | solution.py:45
  170.4 19.1 %all-gather.7.cloned.1.call-done = bf16[2048,1408]{1,0:T(8,128)(2,1)} async-done(((bf16[128,1408]{1,0:T(8,128)(2,1)}), bf16[2048,1408]{1,0:T(8,128)(2,1)}) %all-gather.7.cloned.1.call-update) | async-done | bytes 5767184 | tf_op jit(solution)/shard_map/all_gather | solution.py:207
  189.4 12.0 %fusion.34 = f32[1024,1408]{1,0:T(8,128)} fusion(bf16[2048,1408]{1,0:T(8,128)(2,1)} %all-gather.7.cloned.1.call-done, bf16[1024,2048]{1,0:T(8,128)(2,1)} %get-tuple-element.81, f32[2048]{0:T(1024)S(1)} %convert_element_type.170, f32[1024]{0:T(1024)S(1)} %add_rsqrt_fusion.1), kind=kOutput, calls=%fused_computation.57 | convolution fusion | flops 5913968640 | bytes 15740928 | tf_op jit(solution)/shard_map/dot_general | solution.py:205
  201.4 53.5 %all-gather.11.cloned.1.call-done = bf16[1408,2048]{1,0:T(8,128)(2,1)} async-done(((bf16[1408,128]{1,0:T(8,128)(2,1)}), bf16[1408,2048]{1,0:T(8,128)(2,1)}) %all-gather.11.cloned.1.call-update) | async-done | bytes 5767184 | tf_op jit(solution)/shard_map/all_gather | solution.py:212
  254.9 61.3 %all-gather.9.cloned.1.call-done = bf16[2048,1408]{1,0:T(8,128)(2,1)} async-done(((bf16[128,1408]{1,0:T(8,128)(2,1)}), bf16[2048,1408]{1,0:T(8,128)(2,1)}) %all-gather.9.cloned.1.call-update) | async-done | bytes 5767184 | tf_op jit(solution)/shard_map/all_gather | solution.py:208
  316.1 20.9 %convolution_convert_fusion = bf16[1024,2048]{1,0:T(8,128)(2,1)} fusion(bf16[1408,2048]{1,0:T(8,128)(2,1)} %all-gather.11.cloned.1.call-done, f32[1024,1408]{1,0:T(8,128)} %fusion.34, bf16[2048,1408]{1,0:T(8,128)(2,1)} %all-gather.9.cloned.1.call-done, bf16[1024,2048]{1,0:T(8,128)(2,1)} %get-tuple-element.81, f32[2048]{0:T(1024)S(1)} %convert_element_type.170, ...), kind=kOutput, calls=%fused_computation.36 | convolution fusion | flops 11830296576 | bytes 25702400 | tf_op jit(solution)/shard_map/dot_general | solution.py:210
  337.0 0.0 reduce-scatter.2.cloned.1.call-update
  337.0 1.0 slice.93
  338.1 0.1 fusion.65
  338.1 0.1 copy.70
  338.2 0.7 copy.72
  338.9 4.0 %add_convert_fusion = bf16[16,1,256,512]{3,0,2,1:T(8,128)(2,1)S(1)} fusion(f32[16,1,256,512]{3,0,2,1:T(8,128)} %copy-done.2, f32[256,512]{1,0:T(8,128)S(1)} %bitcast.135, f32[16,256]{0,1:T(8,128)S(1)} %copy.70), kind=kLoop, calls=%fused_computation.18 | loop fusion | flops 6291456 | bytes 13123584 | tf_op jit(solution)/shard_map/convert_element_type | solution.py:219
  342.9 4.4 %copy.71 = bf16[16,1,256,512]{3,2,1,0:T(8,128)(2,1)} copy(bf16[16,1,256,512]{3,0,2,1:T(8,128)(2,1)S(1)} %add_convert_fusion) | data formatting | bytes 8388608
  347.3 4.8 %reduce-scatter.2.cloned.1.call-done = bf16[512,2048]{1,0:T(8,128)(2,1)} async-done(((bf16[1024,2048]{1,0:T(8,128)(2,1)}), bf16[512,2048]{1,0:T(8,128)(2,1)}) %reduce-scatter.2.cloned.1.call-update) | async-done | bytes 2097168 | tf_op jit(solution)/shard_map/reduce_scatter | solution.py:215
  352.1 4.4 %add_convert_fusion.1 = bf16[512,2048]{1,0:T(8,128)(2,1)} fusion(bf16[512,2048]{1,0:T(8,128)(2,1)} %reduce-scatter.2.cloned.1.call-done, bf16[1024,2048]{1,0:T(8,128)(2,1)} %get-tuple-element.81, s32[]{:T(128)S(6)} %select_n.46), kind=kLoop, calls=%fused_computation.35 | loop fusion | flops 4194304 | bytes 6291460 | tf_op jit(solution)/shard_map/convert_element_type | solution.py:218
  (50 shorter events, 0.3 us)
Async XLA Ops:
  8.0 110.5 %copy-start = (bf16[512,2048]{1,0:T(8,128)(2,1)S(1)}, bf16[512,2048]{1,0:T(8,128)(2,1)}, u32[]{:S(2)}) copy-start(bf16[512,2048]{1,0:T(8,128)(2,1)} %param.27) | copy-start | bytes 6291460
  8.0 3.3 copy-start.9
  8.0 97.4 %all-gather.5.cloned.1.call-start = ((), (), s32[]{:S(2)}) async-start(), calls=%async_computation.1 | async-start | bytes 1310720 | tf_op jit(solution)/shard_map/all_gather | solution.py:24
  8.1 3.6 copy-start.6
  11.6 13.0 %copy-start.11 = (s32[1,16]{1,0:T(1,128)S(1)}, s32[1,16]{1,0:T(1,128)}, u32[]{:S(2)}) copy-start(s32[1,16]{1,0:T(1,128)} %param.33) | copy-start | bytes 196
  11.6 13.0 %copy-start.13 = (s32[1,16]{1,0:T(1,128)S(1)}, s32[1,16]{1,0:T(1,128)}, u32[]{:S(2)}) copy-start(s32[1,16]{1,0:T(1,128)} %param.32) | copy-start | bytes 196
  11.6 13.2 %copy-start.8 = (bf16[4,1024]{1,0:T(4,128)(2,1)S(1)}, bf16[4,1024]{1,0:T(4,128)(2,1)}, u32[]{:S(2)}) copy-start(bf16[4,1024]{1,0:T(4,128)(2,1)} %param.21) | copy-start | bytes 24580
  11.6 13.2 %copy-start.14 = (bf16[2048,16]{0,1:T(8,128)(2,1)S(1)}, bf16[2048,16]{0,1:T(8,128)(2,1)}, u32[]{:S(2)}) copy-start(bf16[2048,16]{0,1:T(8,128)(2,1)} %param.22) | copy-start | bytes 196612
  11.6 13.2 %copy-start.15 = (bf16[16,256]{1,0:T(8,128)(2,1)S(1)}, bf16[16,256]{1,0:T(8,128)(2,1)}, u32[]{:S(2)}) copy-start(bf16[16,256]{1,0:T(8,128)(2,1)} %param.23) | copy-start | bytes 24580
  11.7 13.2 %copy-start.16 = (f32[256]{0:T(256)S(1)}, f32[256]{0:T(256)}, u32[]{:S(2)}) copy-start(f32[256]{0:T(256)} %param.24) | copy-start | bytes 3076
  18.9 1.3 copy-start.7
  20.3 25.7 %collective-permute-start = (bf16[3,1024]{1,0:T(4,128)(2,1)S(1)}, bf16[3,1024]{1,0:T(4,128)(2,1)S(1)}, u32[]{:S(2)}, u32[]{:S(2)}) collective-permute-start(bf16[3,1024]{1,0:T(4,128)(2,1)S(1)} %slice_bitcast_fusion.5), channel_id=1, source_target_pairs={{0,2},{2,4},{4,6},{1,3},{3,5},{5,7},{8,10},{10,12},{12,14},{9,11},... | collective-permute-start | bytes 18440 | tf_op jit(solution)/shard_map/ppermute | solution.py:18
  30.0 9.0 %copy-start.12 = (bf16[512]{0:T(512)(128)(2,1)S(1)}, bf16[512]{0:T(512)(128)(2,1)}, u32[]{:S(2)}) copy-start(bf16[512]{0:T(512)(128)(2,1)} %param.26) | copy-start | bytes 3076
  31.9 60.4 %copy-start.5 = (f32[16,1,64,256]{3,0,1,2:T(8,128)}, f32[16,1,64,256]{3,0,1,2:T(8,128)S(1)}, u32[]{:S(2)}) copy-start(f32[16,1,64,256]{3,0,1,2:T(8,128)S(1)} %fusion.48) | copy-start | bytes 3145732
  53.7 7.4 %copy-start.3 = (f32[16,64,1,1024]{3,1,0,2:T(8,128)}, f32[16,64,1,1024]{3,1,0,2:T(8,128)S(1)}, u32[]{:S(2)}) copy-start(f32[16,64,1,1024]{3,1,0,2:T(8,128)S(1)} %fusion.15) | copy-start | bytes 12582916
  74.7 3.2 copy-start.2
  79.3 83.3 %all-reduce.3.cloned.1.call-start = ((), (), s32[]{:S(2)}) async-start(), calls=%async_computation.2 | async-start | bytes 8388608 | tf_op jit(solution)/shard_map/psum | solution.py:199
  79.5 4.2 %copy-start.4 = (f32[16,64,1,1024]{3,1,0,2:T(8,128)S(1)}, f32[16,64,1,1024]{3,1,0,2:T(8,128)}, u32[]{:S(2)}) copy-start(f32[16,64,1,1024]{3,1,0,2:T(8,128)} %copy-done.3) | copy-start | bytes 12582916
  122.9 2.1 copy-start.10
  122.9 66.5 %all-gather.7.cloned.1.call-start = ((), (), s32[]{:S(2)}) async-start(), calls=%async_computation.3 | async-start | bytes 6127616 | tf_op jit(solution)/shard_map/all_gather | solution.py:207
  123.5 131.4 %all-gather.11.cloned.1.call-start = ((), (), s32[]{:S(2)}) async-start(), calls=%async_computation.5 | async-start | bytes 6127616 | tf_op jit(solution)/shard_map/all_gather | solution.py:212
  124.1 192.1 %all-gather.9.cloned.1.call-start = ((), (), s32[]{:S(2)}) async-start(), calls=%async_computation.4 | async-start | bytes 6127616 | tf_op jit(solution)/shard_map/all_gather | solution.py:208
  124.7 227.5 %reduce-scatter.2.cloned.1.call-start = ((), (), s32[]{:S(2)}) async-start(), calls=%async_computation.6 | async-start | bytes 6291456 | tf_op jit(solution)/shard_map/reduce_scatter | solution.py:215
  342.9 13.7 %copy-start.1 = (bf16[512,2048]{1,0:T(8,128)(2,1)S(1)}, bf16[512,2048]{1,0:T(8,128)(2,1)}, u32[]{:S(2)}) copy-start(bf16[512,2048]{1,0:T(8,128)(2,1)} %param.27) | copy-start | bytes 6291460
Sparse Core Ops, SparseCore 0:
  79.4 24.9 all-gather.4
  123.0 39.5 all-reduce.2
  337.2 14.9 reduce-scatter.1
Sparse Core Ops, SparseCore 1:
  125.7 63.6 all-gather.6
  191.6 63.2 all-gather.10
  257.1 59.0 all-gather.8
where the time goes:
time: 371 us; the launch traced here: 364 us
  waiting for transfers between devices  178 us (48%)
  matrix products  104 us (28%)
  other arithmetic  39.8 us (11%)
  between operations  16.3 us (4%)
  local copies, waits for them, and re-layouts  14.4 us (4%)
  blocking collectives  6.9 us (2%)
  starting transfers between devices  5.04 us (1%)
    all_gather x1, waiting for transfers between devices, on_device(): up_part = widen(lax.all_gather(up_weight, 'req', axis=0, tiled=True))  61.3 us
    all_gather x1, waiting for transfers between devices, on_device(): lax.all_gather(down_weight, 'req', axis=1, tiled=True)  53.5 us
    psum x1, waiting for transfers between devices, on_device(): lax.psum(partial_value.astype(jnp.bfloat16), 'hid').astype(jnp.float32)  37.7 us
    dot_general x1, matrix products, on_device(): jnp.dot(hidden, lax.all_gather(down_weight, 'req', axis=1, tiled=True), p...  20.9 us
    all_gather x1, waiting for transfers between devices, on_device(): gate_part = widen(lax.all_gather(gate_weight, 'req', axis=0, tiled=True))  19.1 us
    dot_general x1, matrix products, page_block(): jnp.einsum('pqhe,qheb->pheb', weights, page_terms, precision=TOP_PRECISION)  13.6 us
    dot_general x1, matrix products, page_block(): jnp.einsum('phik,phkv->phiv', raised_rows, previous, precision=TOP_PRECIS...  13.1 us
    dot_general x1, matrix products, widen(): return jnp.dot(feed_in, weight_rows, preferred_element_type=jnp.float32)  12 us
  transfers between devices with their start and end apart: 7, of which 5 were waited for; matrix products, arithmetic and copies ran while one was open for 19% of the time, Pallas kernels for 0%

commit v1 on v0

--- a/solution.py
+++ b/solution.py
@@ -196,7 +196,9 @@
     partial_value = jnp.dot(gated_rows, output_weight, preferred_element_type=jnp.float32)
     half_rows = token_count // lax.axis_size("hid")
     row_start = lax.axis_index("hid") * half_rows
-    mixed_sum = lax.psum(partial_value.astype(jnp.bfloat16), "hid").astype(jnp.float32)
+    mixed_sum = jnp.sum(lax.all_gather(partial_value.astype(jnp.bfloat16), "hid"), axis=0).astype(
+        jnp.float32
+    )
     residual = (tokens.astype(jnp.float32) + mixed_sum).astype(jnp.bfloat16)
     feed_in = rms_scaled(residual, mixer_gain).astype(jnp.bfloat16)
     own_residual = lax.dynamic_slice_in_dim(residual, row_start, half_rows, 0)

time: 371 us -> 393 us (1.059)
  waiting for transfers between devices: 178 us -> 193 us
  other arithmetic: 39.8 us -> 48.4 us
    psum x1 -> x0, waiting for transfers between devices: 37.7 us -> none  [on_device(): lax.psum(partial_value.astype(jnp.bfloat16), 'hid').astype(jnp.float32)]
    all_gather x1, waiting for transfers between devices: 19.1 us -> 45.5 us  [on_device(): gate_part = widen(lax.all_gather(gate_weight, 'req', axis=0, tiled=True))]
    all_gather x0 -> x1, waiting for transfers between devices: none -> 26.1 us  [on_device(): lax.all_gather(partial_value.astype(jnp.bfloat16), 'hid')]
    all_gather x1, waiting for transfers between devices: 61.3 us -> 48.5 us  [on_device(): up_part = widen(lax.all_gather(up_weight, 'req', axis=0, tiled=True))]
    all_gather x1, waiting for transfers between devices: 53.5 us -> 65.9 us  [on_device(): lax.all_gather(down_weight, 'req', axis=1, tiled=True)]
    reduce_sum x0 -> x1, other arithmetic: none -> 8.78 us  [on_device(): jnp.sum(lax.all_gather(partial_value.astype(jnp.bfloat16), 'hid'), axis=0)]
  transfers between devices with their start and end apart: 7 -> 7, of which waited for: 5 -> 5; matrix products, arithmetic and copies ran while one was open for 19% -> 20% of each run, Pallas kernels for 0% -> 0%
where the time goes in v1:
time: 393 us; the launch traced here: 387 us
  waiting for transfers between devices  193 us (49%)
  matrix products  104 us (26%)
  other arithmetic  48.4 us (12%)
  between operations  14.7 us (4%)
  local copies, waits for them, and re-layouts  14.5 us (4%)
  blocking collectives  6.91 us (2%)
  starting transfers between devices  5.21 us (1%)
    all_gather x1, waiting for transfers between devices, on_device(): lax.all_gather(down_weight, 'req', axis=1, tiled=True)  65.9 us
    all_gather x1, waiting for transfers between devices, on_device(): up_part = widen(lax.all_gather(up_weight, 'req', axis=0, tiled=True))  48.5 us
    all_gather x1, waiting for transfers between devices, on_device(): gate_part = widen(lax.all_gather(gate_weight, 'req', axis=0, tiled=True))  45.5 us
    all_gather x1, waiting for transfers between devices, on_device(): lax.all_gather(partial_value.astype(jnp.bfloat16), 'hid')  26.1 us
    dot_general x1, matrix products, on_device(): jnp.dot(hidden, lax.all_gather(down_weight, 'req', axis=1, tiled=True), p...  20.9 us
    dot_general x1, matrix products, page_block(): jnp.einsum('pqhe,qheb->pheb', weights, page_terms, precision=TOP_PRECISION)  13.4 us
    dot_general x1, matrix products, page_block(): jnp.einsum('phik,phkv->phiv', raised_rows, previous, precision=TOP_PRECIS...  13.1 us
    dot_general x1, matrix products, widen(): return jnp.dot(feed_in, weight_rows, preferred_element_type=jnp.float32)  12 us
  transfers between devices with their start and end apart: 7, of which 5 were waited for; matrix products, arithmetic and copies ran while one was open for 20% of the time, Pallas kernels for 0%

profile of v1, /device:TPU:1, one launch (start us, length us, event | category | flops | bytes accessed | tf_op | source)
XLA Modules:
  0.0 386.6 jit_solution(4404167037331040253)
XLA Ops:
  7.2 0.0 all-gather.7.cloned.1.call-start
  7.2 3.2 fusion.3
  10.5 0.3 copy-done.6
  10.8 7.3 %convolution_convert_fusion.2 = bf16[1024,1024]{1,0:T(8,128)(2,1)S(1)} fusion(bf16[2048,1024]{1,0:T(8,128)(2,1)} %param.20, bf16[1024,2048]{1,0:T(8,128)(2,1)S(1)} %copy-done.6, f32[2048]{0:T(1024)S(1)} %convert_element_type.151, f32[1024]{0:T(1024)S(1)} %add_rsqrt_fusion.2), kind=kOutput, calls=%fused_computation.53 | convolution fusion | flops 4304404480 | bytes 10498048 | tf_op jit(solution)/shard_map/dot_general | solution.py:143
  18.1 1.3 copy-done.7
  19.4 4.4 %collective-permute-start = (bf16[3,1024]{1,0:T(4,128)(2,1)S(1)}, bf16[3,1024]{1,0:T(4,128)(2,1)S(1)}, u32[]{:S(2)}, u32[]{:S(2)}) collective-permute-start(bf16[3,1024]{1,0:T(4,128)(2,1)S(1)} %slice_bitcast_fusion.5), channel_id=1, source_target_pairs={{0,2},{2,4},{4,6},{1,3},{3,5},{5,7},{8,10},{10,12},{12,14},{9,11},... | collective-permute-start | bytes 18440 | tf_op jit(solution)/shard_map/ppermute | solution.py:18
  23.9 0.1 select_reduce_fusion
  24.0 5.2 %fusion.37 = f32[1024,256]{1,0:T(8,128)} fusion(bf16[16,256]{1,0:T(8,128)(2,1)S(1)} %copy-done.15, bf16[2048,16]{0,1:T(8,128)(2,1)S(1)} %copy-done.14, f32[256]{0:T(256)S(1)} %copy-done.16, bf16[1024,2048]{1,0:T(8,128)(2,1)} %param.18, f32[2048]{0:T(1024)S(1)} %convert_element_type.151, f32[1024]{0:T(1024)S(1)} %add_rsqrt_fusion.2), kind=kOutput, calls=%fused_computation.60 | convolution fusion | flops 86523904 | bytes 5329920 | tf_op jit(solution)/shard_map/dot_general | solution.py:156
  29.2 1.8 fusion.48
  31.1 0.1 and_convert_fusion
  31.2 0.1 subtract_bitcast_fusion
  31.3 0.1 copy.61
  31.4 0.1 reduce.3
  31.5 0.1 fusion.69
  31.6 0.1 copy.67
  31.7 0.5 slice.90
  32.2 0.7 fusion.71
  32.9 1.0 slice.80
  33.9 4.1 %convert_element_type.154 = f32[16,64,1024]{2,1,0:T(8,128)} convert(bf16[16,64,1024]{2,1,0:T(8,128)(2,1)} %bitcast.140) | non-fusion elementwise | flops 1048576 | bytes 6291456 | tf_op jit(solution)/shard_map/convert_element_type | solution.py:63
  38.0 0.1 copy.75
  38.1 0.1 reduce.4
  38.2 6.9 %all_gather.23 = bf16[4,1,256]{2,1,0:T(2,128)(2,1)S(1)} all-gather(bf16[1,1,256]{2,1,0:T(2,128)(2,1)S(1)} %fusion.71), channel_id=1, replica_groups=mesh['req'=16,'seq'=4,'hid'=2] {'seq'}, dimensions={0}, use_global_device_ids=true | all-gather | bytes 2560 | tf_op jit(solution)/shard_map/all_gather | solution.py:24
  45.1 0.1 convert_multiply_fusion.4
  45.2 7.6 %fusion.15 = f32[16,64,1,1024]{3,1,0,2:T(8,128)S(1)} fusion(f32[16,64,1024]{2,1,0:T(8,128)} %convert_element_type.154, f32[16,3,1024]{2,1,0:T(4,128)S(1)} %convert_multiply_fusion.4, f32[1024]{0:T(1024)S(1)} %bitcast.147, f32[1024]{0:T(1024)S(1)} %bitcast.148, f32[1024]{0:T(1024)S(1)} %bitcast.146, f32[1024]{0:T(1024)S(1)} %bitcast.145), kind=kLoop, calls=%fused_computation.29 | loop fusion | flops 10485760 | bytes 8601600 | tf_op jit(solution)/shard_map/reshape | solution.py:149
  52.9 7.4 %fusion.30 = f32[16,256,512]{2,1,0:T(8,128)S(1)} fusion(f32[16,64,1,1024]{3,1,0,2:T(8,128)S(1)} %fusion.15, f32[16,1,64,256]{3,0,1,2:T(8,128)S(1)} %fusion.48, f32[16,256]{1,0:T(8,128)S(1)} %get-tuple-element.85), kind=kOutput, calls=%fused_computation.51 | convolution fusion | flops 1612447744 | bytes 12599296 | tf_op jit(solution)/shard_map/phte,phtb->pheb/dot_general | solution.py:99
  60.3 13.4 %fusion.20 = f32[16,1,256,512]{3,0,2,1:T(8,128)S(1)} fusion(f32[16,256,512]{2,1,0:T(8,128)S(1)} %fusion.30, f32[16,256]{0,1:T(8,128)S(1)} %bitcast.142, pred[16,16]{1,0:T(8,128)(4,1)S(1)} %fusion.69), kind=kOutput, calls=%fused_computation.38 | convolution fusion | flops 402849792 | bytes 16793856 | tf_op jit(solution)/shard_map/pqhe,qheb->pheb/dot_general | solution.py:107
  73.7 3.2 copy-done.2
  76.9 0.6 slice.154
  77.5 0.8 copy.68
  78.2 0.0 all-gather.7.cloned.1.call-update
  78.3 0.4 all-gather.15.cloned.1.call-start
  78.7 4.2 %convolution_select_fusion = f32[16,64,64]{2,1,0:T(8,128)S(1)} fusion(f32[16,1,64,256]{3,0,1,2:T(8,128)S(1)} %fusion.48, pred[64,64]{1,0:T(8,128)(4,1)S(1)} %iota_compare_fusion, f32[16,64,1,1024]{3,1,0,2:T(8,128)} %copy-done.3), kind=kOutput, calls=%fused_computation.56 | convolution fusion | flops 204537856 | bytes 4464640 | tf_op jit(solution)/shard_map/phik,phjk->phij/dot_general | solution.py:92
  83.0 3.1 fusion.31
  86.1 5.4 %multiply_bitcast_fusion = f32[16,256,512]{2,0,1:T(8,128)S(1)} fusion(f32[15,1,256,512]{3,0,2,1:T(8,128)} %bitcast.135, f32[16]{0:T(128)S(1)} %get-tuple-element.83), kind=kLoop, calls=%fused_computation.19 | loop fusion | flops 2097152 | bytes 16252992 | tf_op jit(solution)/shard_map/reshape.33
  91.5 13.1 %fusion.7 = f32[16,64,512]{2,1,0:T(8,128)} fusion(f32[16,256,512]{2,0,1:T(8,128)S(1)} %multiply_bitcast_fusion, f32[16,1,64,256]{3,0,1,2:T(8,128)S(1)} %fusion.48, f32[16,64,1,1024]{3,1,0,2:T(8,128)} %copy-done.3), kind=kOutput, calls=%fused_computation.14 | convolution fusion | flops 1611923456 | bytes 12582912 | tf_op jit(solution)/shard_map/phik,phkv->phiv/dot_general | solution.py:110
  104.6 6.8 %multiply_reduce_fusion = (f32[16,64]{1,0:T(8,128)S(1)}, f32[16,1,64,512]{3,2,0,1:T(8,128)}) fusion(f32[16,1,64,256]{3,0,1,2:T(8,128)} %copy-done.5, f32[16,256]{1,0:T(8,128)S(1)} %get-tuple-element.84, f32[16]{0:T(128)S(1)} %reduce.4, f32[16,64,1,1024]{3,1,0,2:T(8,128)} %copy-done.3, f32[1,256,512]{2,1,0:T(8,128)S(1)} %get-tuple-element.47, ...), kind=kOutput, calls=%fused_computation.46 | convolution fusion | flops 1614543872 | bytes 8933440 | tf_op jit(solution)/shard_map/dlof,lfg->dlog/dot_general | solution.py:182
  111.4 0.1 rsqrt.29
  111.5 6.2 %fusion.25 = bf16[1024,512]{1,0:T(8,128)(2,1)S(1)} fusion(f32[16,1,64,512]{3,2,0,1:T(8,128)} %get-tuple-element.91, f32[512]{0:T(512)S(1)} %convert_element_type.165, f32[1024]{0:T(1024)S(1)} %rsqrt.29, bf16[2048,512]{1,0:T(8,128)(2,1)} %param.25, bf16[1024,2048]{1,0:T(8,128)(2,1)} %param.18, f32[2048]{0:T(1024)S(1)} %convert_element_type.151, ...), kind=kOutput, calls=%fused_computation.45 | convolution fusion | flops 2160066560 | bytes 9455616 | tf_op jit(solution)/shard_map/dot_general | solution.py:190
  117.7 4.4 %convolution_convert_fusion.1 = bf16[1024,2048]{1,0:T(8,128)(2,1)} fusion(bf16[1024,512]{1,0:T(8,128)(2,1)S(1)} %fusion.25, bf16[512,2048]{1,0:T(8,128)(2,1)S(1)} %copy-done), kind=kOutput, calls=%fused_computation.37 | convolution fusion | flops 2149580800 | bytes 7340032 | tf_op jit(solution)/shard_map/dot_general | solution.py:196
  122.0 0.0 all-gather.15.cloned.1.call-update
  122.1 0.0 all-gather.9.cloned.1.call-start
  122.1 0.7 all-gather.9.cloned.1.call-update
  122.8 0.0 all-gather.11.cloned.1.call-start
  122.8 0.5 all-gather.11.cloned.1.call-update
  123.4 0.0 all-gather.13.cloned.1.call-start
  123.4 0.5 all-gather.13.cloned.1.call-update
  124.0 0.3 reduce-scatter.2.cloned.1.call-start
  124.2 26.1 %all-gather.15.cloned.1.call-done = bf16[2048,2048]{1,0:T(8,128)(2,1)} async-done(((bf16[1024,2048]{1,0:T(8,128)(2,1)}), bf16[2048,2048]{1,0:T(8,128)(2,1)}) %all-gather.15.cloned.1.call-update) | async-done | bytes 8388624 | tf_op jit(solution)/shard_map/all_gather | solution.py:199
  150.4 8.8 %reduce_sum.51 = bf16[1024,2048]{1,0:T(8,128)(2,1)} reduce(bf16[2,1024,2048]{2,1,0:T(8,128)(2,1)} %bitcast.137, bf16[]{:T(256)} %constant.84.clone.1), dimensions={0}, to_apply=%region_9.10 | reduce | flops 2097152 | bytes 12582914 | tf_op jit(solution)/shard_map/reduce_sum | solution.py:199
  159.2 7.5 %fusion = (f32[1024]{0:T(1024)S(1)}, bf16[1024,2048]{1,0:T(8,128)(2,1)}) fusion(bf16[1024,2048]{1,0:T(8,128)(2,1)} %reduce_sum.51, bf16[1024,2048]{1,0:T(8,128)(2,1)} %param.18), kind=kLoop, calls=%fused_computation.7 | loop fusion | flops 14679040 | bytes 12587008 | tf_op jit(solution)/shard_map/reduce_sum | solution.py:45
  166.7 45.5 %all-gather.9.cloned.1.call-done = bf16[2048,1408]{1,0:T(8,128)(2,1)} async-done(((bf16[128,1408]{1,0:T(8,128)(2,1)}), bf16[2048,1408]{1,0:T(8,128)(2,1)}) %all-gather.9.cloned.1.call-update) | async-done | bytes 5767184 | tf_op jit(solution)/shard_map/all_gather | solution.py:209
  212.2 12.0 %fusion.34 = f32[1024,1408]{1,0:T(8,128)} fusion(bf16[2048,1408]{1,0:T(8,128)(2,1)} %all-gather.9.cloned.1.call-done, bf16[1024,2048]{1,0:T(8,128)(2,1)} %get-tuple-element.81, f32[2048]{0:T(1024)S(1)} %convert_element_type.172, f32[1024]{0:T(1024)S(1)} %add_rsqrt_fusion.1), kind=kOutput, calls=%fused_computation.57 | convolution fusion | flops 5913968640 | bytes 15740928 | tf_op jit(solution)/shard_map/dot_general | solution.py:207
  224.2 48.5 %all-gather.11.cloned.1.call-done = bf16[2048,1408]{1,0:T(8,128)(2,1)} async-done(((bf16[128,1408]{1,0:T(8,128)(2,1)}), bf16[2048,1408]{1,0:T(8,128)(2,1)}) %all-gather.11.cloned.1.call-update) | async-done | bytes 5767184 | tf_op jit(solution)/shard_map/all_gather | solution.py:210
  272.7 65.9 %all-gather.13.cloned.1.call-done = bf16[1408,2048]{1,0:T(8,128)(2,1)} async-done(((bf16[1408,128]{1,0:T(8,128)(2,1)}), bf16[1408,2048]{1,0:T(8,128)(2,1)}) %all-gather.13.cloned.1.call-update) | async-done | bytes 5767184 | tf_op jit(solution)/shard_map/all_gather | solution.py:214
  338.6 20.9 %convolution_convert_fusion = bf16[1024,2048]{1,0:T(8,128)(2,1)} fusion(bf16[1408,2048]{1,0:T(8,128)(2,1)} %all-gather.13.cloned.1.call-done, f32[1024,1408]{1,0:T(8,128)} %fusion.34, bf16[2048,1408]{1,0:T(8,128)(2,1)} %all-gather.11.cloned.1.call-done, bf16[1024,2048]{1,0:T(8,128)(2,1)} %get-tuple-element.81, f32[2048]{0:T(1024)S(1)} %convert_element_type.172, ...), kind=kOutput, calls=%fused_computation.36 | convolution fusion | flops 11830296576 | bytes 25702400 | tf_op jit(solution)/shard_map/dot_general | solution.py:212
  359.5 0.0 reduce-scatter.2.cloned.1.call-update
  359.6 1.0 slice.93
  360.6 0.1 fusion.65
  360.7 0.1 copy.70
  360.8 0.7 copy.72
  361.4 4.0 %add_convert_fusion = bf16[16,1,256,512]{3,0,2,1:T(8,128)(2,1)S(1)} fusion(f32[16,1,256,512]{3,0,2,1:T(8,128)} %copy-done.2, f32[256,512]{1,0:T(8,128)S(1)} %bitcast.136, f32[16,256]{0,1:T(8,128)S(1)} %copy.70), kind=kLoop, calls=%fused_computation.18 | loop fusion | flops 6291456 | bytes 13123584 | tf_op jit(solution)/shard_map/convert_element_type | solution.py:221
  365.4 4.5 %copy.71 = bf16[16,1,256,512]{3,2,1,0:T(8,128)(2,1)} copy(bf16[16,1,256,512]{3,0,2,1:T(8,128)(2,1)S(1)} %add_convert_fusion) | data formatting | bytes 8388608
  369.9 5.2 %reduce-scatter.2.cloned.1.call-done = bf16[512,2048]{1,0:T(8,128)(2,1)} async-done(((bf16[1024,2048]{1,0:T(8,128)(2,1)}), bf16[512,2048]{1,0:T(8,128)(2,1)}) %reduce-scatter.2.cloned.1.call-update) | async-done | bytes 2097168 | tf_op jit(solution)/shard_map/reduce_scatter | solution.py:217
  375.1 4.4 %add_convert_fusion.1 = bf16[512,2048]{1,0:T(8,128)(2,1)} fusion(bf16[512,2048]{1,0:T(8,128)(2,1)} %reduce-scatter.2.cloned.1.call-done, bf16[1024,2048]{1,0:T(8,128)(2,1)} %get-tuple-element.81, s32[]{:T(128)S(6)} %select_n.46), kind=kLoop, calls=%fused_computation.35 | loop fusion | flops 4194304 | bytes 6291460 | tf_op jit(solution)/shard_map/convert_element_type | solution.py:220
  (51 shorter events, 0.3 us)
Async XLA Ops:
  7.2 110.5 %copy-start = (bf16[512,2048]{1,0:T(8,128)(2,1)S(1)}, bf16[512,2048]{1,0:T(8,128)(2,1)}, u32[]{:S(2)}) copy-start(bf16[512,2048]{1,0:T(8,128)(2,1)} %param.27) | copy-start | bytes 6291460
  7.2 3.3 copy-start.9
  7.2 97.4 %all-gather.7.cloned.1.call-start = ((), (), s32[]{:S(2)}) async-start(), calls=%async_computation.1 | async-start | bytes 1310720 | tf_op jit(solution)/shard_map/all_gather | solution.py:24
  7.2 3.6 copy-start.6
  10.8 13.0 %copy-start.11 = (s32[1,16]{1,0:T(1,128)S(1)}, s32[1,16]{1,0:T(1,128)}, u32[]{:S(2)}) copy-start(s32[1,16]{1,0:T(1,128)} %param.33) | copy-start | bytes 196
  10.8 13.0 %copy-start.13 = (s32[1,16]{1,0:T(1,128)S(1)}, s32[1,16]{1,0:T(1,128)}, u32[]{:S(2)}) copy-start(s32[1,16]{1,0:T(1,128)} %param.32) | copy-start | bytes 196
  10.8 13.2 %copy-start.8 = (bf16[4,1024]{1,0:T(4,128)(2,1)S(1)}, bf16[4,1024]{1,0:T(4,128)(2,1)}, u32[]{:S(2)}) copy-start(bf16[4,1024]{1,0:T(4,128)(2,1)} %param.21) | copy-start | bytes 24580
  10.8 13.2 %copy-start.14 = (bf16[2048,16]{0,1:T(8,128)(2,1)S(1)}, bf16[2048,16]{0,1:T(8,128)(2,1)}, u32[]{:S(2)}) copy-start(bf16[2048,16]{0,1:T(8,128)(2,1)} %param.22) | copy-start | bytes 196612
  10.8 13.2 %copy-start.15 = (bf16[16,256]{1,0:T(8,128)(2,1)S(1)}, bf16[16,256]{1,0:T(8,128)(2,1)}, u32[]{:S(2)}) copy-start(bf16[16,256]{1,0:T(8,128)(2,1)} %param.23) | copy-start | bytes 24580
  10.8 13.2 %copy-start.16 = (f32[256]{0:T(256)S(1)}, f32[256]{0:T(256)}, u32[]{:S(2)}) copy-start(f32[256]{0:T(256)} %param.24) | copy-start | bytes 3076
  18.1 1.3 copy-start.7
  19.4 25.7 %collective-permute-start = (bf16[3,1024]{1,0:T(4,128)(2,1)S(1)}, bf16[3,1024]{1,0:T(4,128)(2,1)S(1)}, u32[]{:S(2)}, u32[]{:S(2)}) collective-permute-start(bf16[3,1024]{1,0:T(4,128)(2,1)S(1)} %slice_bitcast_fusion.5), channel_id=1, source_target_pairs={{0,2},{2,4},{4,6},{1,3},{3,5},{5,7},{8,10},{10,12},{12,14},{9,11},... | collective-permute-start | bytes 18440 | tf_op jit(solution)/shard_map/ppermute | solution.py:18
  29.2 9.0 %copy-start.12 = (bf16[512]{0:T(512)(128)(2,1)S(1)}, bf16[512]{0:T(512)(128)(2,1)}, u32[]{:S(2)}) copy-start(bf16[512]{0:T(512)(128)(2,1)} %param.26) | copy-start | bytes 3076
  31.0 60.4 %copy-start.5 = (f32[16,1,64,256]{3,0,1,2:T(8,128)}, f32[16,1,64,256]{3,0,1,2:T(8,128)S(1)}, u32[]{:S(2)}) copy-start(f32[16,1,64,256]{3,0,1,2:T(8,128)S(1)} %fusion.48) | copy-start | bytes 3145732
  52.9 7.4 %copy-start.3 = (f32[16,64,1,1024]{3,1,0,2:T(8,128)}, f32[16,64,1,1024]{3,1,0,2:T(8,128)S(1)}, u32[]{:S(2)}) copy-start(f32[16,64,1,1024]{3,1,0,2:T(8,128)S(1)} %fusion.15) | copy-start | bytes 12582916
  73.7 3.2 copy-start.2
  78.3 72.1 %all-gather.15.cloned.1.call-start = ((), (), s32[]{:S(2)}) async-start(), calls=%async_computation.6 | async-start | bytes 12582912 | tf_op jit(solution)/shard_map/all_gather | solution.py:199
  78.7 4.2 %copy-start.4 = (f32[16,64,1,1024]{3,1,0,2:T(8,128)S(1)}, f32[16,64,1,1024]{3,1,0,2:T(8,128)}, u32[]{:S(2)}) copy-start(f32[16,64,1,1024]{3,1,0,2:T(8,128)} %copy-done.3) | copy-start | bytes 12582916
  122.0 2.2 copy-start.10
  122.1 90.1 %all-gather.9.cloned.1.call-start = ((), (), s32[]{:S(2)}) async-start(), calls=%async_computation.2 | async-start | bytes 6127616 | tf_op jit(solution)/shard_map/all_gather | solution.py:209
  122.8 149.9 %all-gather.11.cloned.1.call-start = ((), (), s32[]{:S(2)}) async-start(), calls=%async_computation.3 | async-start | bytes 6127616 | tf_op jit(solution)/shard_map/all_gather | solution.py:210
  123.4 215.2 %all-gather.13.cloned.1.call-start = ((), (), s32[]{:S(2)}) async-start(), calls=%async_computation.4 | async-start | bytes 6127616 | tf_op jit(solution)/shard_map/all_gather | solution.py:214
  124.0 251.1 %reduce-scatter.2.cloned.1.call-start = ((), (), s32[]{:S(2)}) async-start(), calls=%async_computation.5 | async-start | bytes 6291456 | tf_op jit(solution)/shard_map/reduce_scatter | solution.py:217
  365.4 14.1 %copy-start.1 = (bf16[512,2048]{1,0:T(8,128)(2,1)S(1)}, bf16[512,2048]{1,0:T(8,128)(2,1)}, u32[]{:S(2)}) copy-start(bf16[512,2048]{1,0:T(8,128)(2,1)} %param.27) | copy-start | bytes 6291460
Sparse Core Ops, SparseCore 0:
  78.4 24.9 all-gather.6
  122.2 28.1 all-gather.14
  152.5 59.6 all-gather.8
  214.2 58.4 all-gather.10
  274.6 63.9 all-gather.12
  359.7 15.3 reduce-scatter.1
